TPU v7x, 256 devices: a whole 4x4x8 slice. The times are simulated.
256 devices in a mesh: gx: 16 (over x_lo, y, core), yz: 16 (over z, x_hi).
Axes of the slice: x: 4 (x_hi: 2, x_lo: 2; x = x_hi * 2 + x_lo), y: 4, z: 8, core: 2. Of those that a mesh axis runs over, the one named last changes fastest.
Arguments:
- volume: bfloat16 [128, 16, 128, 128], P('gx', None, 'yz'), may hold values from -6 to 6
- weight_one: bfloat16 [32, 432], replicated, may hold values from -0.875 to 0.875
- weight_two: bfloat16 [64, 864], replicated, may hold values from -0.625 to 0.625
- weight_three: bfloat16 [128, 1728], replicated, may hold values from -0.21875 to 0.21875
Outputs:
- features: bfloat16 [128, 32, 1024], P('yz', 'gx')
All inputs are finite; a program needn't handle non-finite values.
Results may differ from a plain program's by a relative error of at most 0.0053.
Values may be sent and summed in bfloat16 or wider, within the bound.
A program may use at most 64 MiB of HBM per device.

v0:
```python
import jax
import jax.numpy as jnp
from jax import lax
from jax.sharding import PartitionSpec as P


def with_halo(block, sides, width):
    for axis, dim in sides:
        count = lax.axis_size(axis)
        forward = [(i, i + 1) for i in range(count - 1)]
        backward = [(target, source) for source, target in forward]
        low = lax.ppermute(
            lax.slice_in_dim(block, block.shape[dim] - width, None, axis=dim), axis, forward
        )
        high = lax.ppermute(lax.slice_in_dim(block, 0, width, axis=dim), axis, backward)
        block = jnp.concatenate([low, block, high], axis=dim)
    return block


def block_conv(padded, weight):
    in_rows = weight.shape[1] // 27
    kernel = weight.reshape(weight.shape[0], 3, 3, 3, in_rows)
    result = lax.conv_general_dilated(
        padded[None],
        kernel,
        (1, 1, 1),
        "VALID",
        dimension_numbers=("NDCHW", "ODHWI", "NDCHW"),
        preferred_element_type=jnp.float32,
    )
    return result[0]


def conv_pool(padded, weight):
    activated = jax.nn.relu(block_conv(padded, weight))
    planes, rows, height, breadth = activated.shape
    grouped = activated.reshape(planes // 2, 2, rows, height // 2, 2, breadth // 2, 2)
    return (jnp.sum(grouped, axis=(1, 4, 6)) * 0.125).astype(jnp.bfloat16)


def conv_planes(padded, weight):
    result = block_conv(padded, weight)
    planes, rows, height, breadth = result.shape
    return result.reshape(planes, rows, height * breadth)


def face_cells(block):
    grown = with_halo(block, (("gx", 0), ("yz", 2)), 1)
    return jnp.pad(grown, ((0, 0), (0, 0), (0, 0), (1, 1)))


def per_device(volume, weight_one, weight_two, weight_three):
    pooled_one = conv_pool(face_cells(volume), weight_one)
    pooled_two = conv_pool(face_cells(pooled_one), weight_two)
    shards = lax.axis_size("yz")
    out_rows = weight_three.shape[0] // shards
    grown = with_halo(pooled_two, (("gx", 0),), 1)
    whole = lax.all_gather(grown, "yz", axis=2, tiled=True)
    whole = jnp.pad(whole, ((0, 0), (0, 0), (1, 1), (1, 1)))
    picked = lax.dynamic_slice_in_dim(weight_three, lax.axis_index("yz") * out_rows, out_rows, 0)
    summed = jnp.moveaxis(conv_planes(whole, picked), 0, 1)
    return jax.nn.relu(summed).astype(jnp.bfloat16)


def solution(mesh):
    placed = (P("gx", None, "yz", None), P(), P(), P())
    return jax.shard_map(
        per_device, mesh=mesh, in_specs=placed, out_specs=P("yz", "gx", None), check_vma=False
    )
```

profile of v0, /device:TPU:2, one launch (start us, length us, event | category | flops | bytes accessed | tf_op | source)
XLA Modules:
  0.0 144.3 jit_solution(10215442351459870463)
XLA Ops:
  0.8 1.9 %collective-permute-start = (bf16[1,16,8,128]{3,2,1,0:T(8,128)(2,1)S(1)}, bf16[1,16,8,128]{3,2,1,0:T(8,128)(2,1)S(1)}, u32[]{:S(2)}, u32[]{:S(2)}) collective-permute-start(bf16[1,16,8,128]{3,2,1,0:T(8,128)(2,1)S(1)} %get-tuple-element.12), channel_id=1, source_target_pairs={{0,16},{16,32},{32,48},{48,64},{64,80},{80,96},{96,112},{112,128},... | collective-permute-start | bytes 98312 | tf_op jit(solution)/shard_map/ppermute | solution.py:12
  2.8 5.8 %collective-permute-start.1 = (bf16[1,16,8,128]{3,2,1,0:T(8,128)(2,1)S(1)}, bf16[1,16,8,128]{3,2,1,0:T(8,128)(2,1)S(1)}, u32[]{:S(2)}, u32[]{:S(2)}) collective-permute-start(bf16[1,16,8,128]{3,2,1,0:T(8,128)(2,1)S(1)} %get-tuple-element.11), channel_id=1, source_target_pairs={{16,0},{32,16},{48,32},{64,48},{80,64},{96,80},{112,96},{128,112},... | collective-permute-start | bytes 98312 | tf_op jit(solution)/shard_map/ppermute | solution.py:15
  10.2 4.0 %collective-permute-start.2 = (bf16[10,16,1,128]{3,2,1,0:T(2,128)(2,1)S(1)}, bf16[10,16,1,128]{3,2,1,0:T(2,128)(2,1)S(1)}, u32[]{:S(2)}, u32[]{:S(2)}) collective-permute-start(bf16[10,16,1,128]{3,2,1,0:T(2,128)(2,1)S(1)} %get-tuple-element.7), channel_id=1, source_target_pairs={{0,1},{1,2},{2,3},{3,4},{4,5},{5,6},{6,7},{7,8},{8,9},{9,10},{10,1... | collective-permute-start | bytes 122888 | tf_op jit(solution)/shard_map/ppermute | solution.py:12
  14.3 1.3 collective-permute-start.3
  16.5 5.6 %collective-permute-done.3 = bf16[10,16,1,128]{3,2,1,0:T(2,128)(2,1)S(1)} collective-permute-done((bf16[10,16,1,128]{3,2,1,0:T(2,128)(2,1)S(1)}, bf16[10,16,1,128]{3,2,1,0:T(2,128)(2,1)S(1)}, u32[]{:S(2)}, u32[]{:S(2)}) %collective-permute-start.3) | collective-permute-done | bytes 40992 | tf_op jit(solution)/shard_map/ppermute | solution.py:15
  22.1 1.2 fusion.35
  23.6 3.7 %reshape.59 = bf16[10,16,10,1,8,17]{5,4,2,1,0,3:T(8,128)(2,1)} reshape(bf16[10,16,10,1,136]{4,2,1,0,3:T(8,128)(2,1)S(1)} %pad.15) | data formatting | bytes 870400 | tf_op jit(solution)/shard_map/conv_general_dilated | solution.py:23
  27.3 7.9 %copy.58 = bf16[10,16,10,1,8,17]{1,4,5,2,0,3:T(8,128)(2,1)} copy(bf16[10,16,10,1,8,17]{5,4,2,1,0,3:T(8,128)(2,1)} %reshape.59) | data formatting | bytes 870400 | tf_op jit(solution)/shard_map/conv_general_dilated | solution.py:23
  36.4 7.3 %select_maximum_fusion = f32[8,8,8,17,32]{4,2,3,1,0:T(8,128)S(1)} fusion(pred[8,17]{0,1:T(8,128)(4,1)S(1)} %copy-done.2, bf16[32,3,3,3,16]{0,4,3,2,1:T(8,128)(2,1)S(1)} %bitcast.57, bf16[10,16,10,1,7,2]{1,4,5,2,0,3:T(8,128)(2,1)S(1)} %slice.48, bf16[10,16,10,1,8,17]{1,4,5,2,0,3:T(8,128)(2,1)} %copy.58), kind=kOutput, calls=%fused_computation.2 | convolution fusion | flops 242664448 | bytes 1621896 | tf_op jit(solution)/shard_map/conv_general_dilated | solution.py:23
  44.5 2.2 %slice.49 = f32[8,8,1,128,32]{4,1,3,0,2:T(8,128)} slice(f32[8,8,1,136,32]{4,1,3,0,2:T(8,128)S(1)} %bitcast.47), slice={[0:8], [0:8], [0:1], [0:128], [0:32]} | slice | bytes 2097152 | tf_op jit(solution)/shard_map/jit(relu)/max | solution.py:35
  46.7 5.0 %reduce_sum.18 = f32[4,32,4,64]{1,2,3,0:T(4,128)S(1)} reduce(f32[4,2,32,4,2,64,2]{2,4,3,6,5,1,0:T(2,128)} %bitcast.48, f32[]{:T(128)} %constant.8.clone.1), dimensions={1,4,6}, to_apply=%region_0.1 | reduce | flops 229376 | bytes 1179652 | tf_op jit(solution)/shard_map/reduce_sum | solution.py:38
  51.9 1.9 %collective-permute-start.4 = (bf16[1,32,4,64]{1,2,3,0:T(4,128)(2,1)S(1)}, bf16[1,32,4,64]{1,2,3,0:T(4,128)(2,1)S(1)}, u32[]{:S(2)}, u32[]{:S(2)}) collective-permute-start(bf16[1,32,4,64]{1,2,3,0:T(4,128)(2,1)S(1)} %get-tuple-element.9), channel_id=1, source_target_pairs={{0,16},{16,32},{32,48},{48,64},{64,80},{80,96},{96,112},{112,128},... | collective-permute-start | bytes 49160 | tf_op jit(solution)/shard_map/ppermute | solution.py:12
  53.8 5.8 %collective-permute-start.5 = (bf16[1,32,4,64]{1,2,3,0:T(4,128)(2,1)S(1)}, bf16[1,32,4,64]{1,2,3,0:T(4,128)(2,1)S(1)}, u32[]{:S(2)}, u32[]{:S(2)}) collective-permute-start(bf16[1,32,4,64]{1,2,3,0:T(4,128)(2,1)S(1)} %get-tuple-element.10), channel_id=1, source_target_pairs={{16,0},{32,16},{48,32},{64,48},{80,64},{96,80},{112,96},{128,112},... | collective-permute-start | bytes 49160 | tf_op jit(solution)/shard_map/ppermute | solution.py:15
  59.6 1.9 %collective-permute-done.5 = bf16[1,32,4,64]{1,2,3,0:T(4,128)(2,1)S(1)} collective-permute-done((bf16[1,32,4,64]{1,2,3,0:T(4,128)(2,1)S(1)}, bf16[1,32,4,64]{1,2,3,0:T(4,128)(2,1)S(1)}, u32[]{:S(2)}, u32[]{:S(2)}) %collective-permute-start.5) | collective-permute-done | bytes 16416 | tf_op jit(solution)/shard_map/ppermute | solution.py:15
  62.1 5.8 %collective-permute-start.6 = (bf16[6,32,1,64]{1,2,3,0:T(2,128)(2,1)S(1)}, bf16[6,32,1,64]{1,2,3,0:T(2,128)(2,1)S(1)}, u32[]{:S(2)}, u32[]{:S(2)}) collective-permute-start(bf16[6,32,1,64]{1,2,3,0:T(2,128)(2,1)S(1)} %get-tuple-element.5), channel_id=1, source_target_pairs={{0,1},{1,2},{2,3},{3,4},{4,5},{5,6},{6,7},{7,8},{8,9},{9,10},{10,1... | collective-permute-start | bytes 73736 | tf_op jit(solution)/shard_map/ppermute | solution.py:12
  67.9 1.3 collective-permute-start.7
  69.6 3.6 %collective-permute-done.6 = bf16[6,32,1,64]{1,2,3,0:T(2,128)(2,1)S(1)} collective-permute-done((bf16[6,32,1,64]{1,2,3,0:T(2,128)(2,1)S(1)}, bf16[6,32,1,64]{1,2,3,0:T(2,128)(2,1)S(1)}, u32[]{:S(2)}, u32[]{:S(2)}) %collective-permute-start.6) | collective-permute-done | bytes 24608 | tf_op jit(solution)/shard_map/ppermute | solution.py:12
  73.3 3.6 %collective-permute-done.7 = bf16[6,32,1,64]{1,2,3,0:T(2,128)(2,1)S(1)} collective-permute-done((bf16[6,32,1,64]{1,2,3,0:T(2,128)(2,1)S(1)}, bf16[6,32,1,64]{1,2,3,0:T(2,128)(2,1)S(1)}, u32[]{:S(2)}, u32[]{:S(2)}) %collective-permute-start.7) | collective-permute-done | bytes 24608 | tf_op jit(solution)/shard_map/ppermute | solution.py:15
  78.2 1.4 fusion.36
  80.3 1.9 %collective-permute-start.8 = (bf16[1,64,2,32]{1,2,3,0:T(2,128)(2,1)S(1)}, bf16[1,64,2,32]{1,2,3,0:T(2,128)(2,1)S(1)}, u32[]{:S(2)}, u32[]{:S(2)}) collective-permute-start(bf16[1,64,2,32]{1,2,3,0:T(2,128)(2,1)S(1)} %get-tuple-element.13), channel_id=1, source_target_pairs={{0,16},{16,32},{32,48},{48,64},{64,80},{80,96},{96,112},{112,128},... | collective-permute-start | bytes 24584 | tf_op jit(solution)/shard_map/ppermute | solution.py:12
  82.2 5.8 %collective-permute-start.9 = (bf16[1,64,2,32]{1,2,3,0:T(2,128)(2,1)S(1)}, bf16[1,64,2,32]{1,2,3,0:T(2,128)(2,1)S(1)}, u32[]{:S(2)}, u32[]{:S(2)}) collective-permute-start(bf16[1,64,2,32]{1,2,3,0:T(2,128)(2,1)S(1)} %get-tuple-element.14), channel_id=1, source_target_pairs={{16,0},{32,16},{48,32},{64,48},{80,64},{96,80},{112,96},{128,112},... | collective-permute-start | bytes 24584 | tf_op jit(solution)/shard_map/ppermute | solution.py:15
  88.2 1.2 collective-permute-done.9
  89.5 48.7 %all_gather.3 = bf16[4,64,32,32]{1,3,0,2:T(8,128)(2,1)S(1)} all-gather(bf16[4,64,2,32]{1,3,0,2:T(8,128)(2,1)S(1)} %copy.69), channel_id=1, replica_groups=mesh['gx'=16,'yz'=16] {'yz'}, dimensions={2}, use_global_device_ids=true | all-gather | bytes 557056 | tf_op jit(solution)/shard_map/all_gather | solution.py:58
  140.2 2.7 %fusion.30 = bf16[2,32,8,5,8]{4,2,3,1,0:T(8,128)(2,1)S(1)} fusion(bf16[8,3,3,3,64]{0,4,3,2,1:T(8,128)(2,1)S(1)} %bitcast.54, bf16[4,64,34,1,7,2]{1,4,5,2,0,3:T(8,128)(2,1)S(1)} %slice.58, bf16[4,64,34,1,8,5]{1,4,5,2,0,3:T(8,128)(2,1)S(1)} %copy.72, pred[8,5]{0,1:T(8,128)(4,1)S(1)} %copy-done.4), kind=kOutput, calls=%fused_computation.29 | convolution fusion | flops 73764864 | bytes 1008680 | tf_op jit(solution)/shard_map/conv_general_dilated | solution.py:23
  (55 shorter events, 12.5 us)
Async XLA Ops:
  0.0 88.0 %copy-start = (bf16[128,1728]{0,1:T(8,128)(2,1)S(1)}, bf16[128,1728]{0,1:T(8,128)(2,1)}, u32[]{:S(2)}) copy-start(bf16[128,1728]{0,1:T(8,128)(2,1)} %param.7) | copy-start | bytes 1327108
  0.8 7.7 %collective-permute-start = (bf16[1,16,8,128]{3,2,1,0:T(8,128)(2,1)S(1)}, bf16[1,16,8,128]{3,2,1,0:T(8,128)(2,1)S(1)}, u32[]{:S(2)}, u32[]{:S(2)}) collective-permute-start(bf16[1,16,8,128]{3,2,1,0:T(8,128)(2,1)S(1)} %get-tuple-element.12), channel_id=1, source_target_pairs={{0,16},{16,32},{32,48},{48,64},{64,80},{80,96},{96,112},{112,128},... | collective-permute-start | bytes 98312 | tf_op jit(solution)/shard_map/ppermute | solution.py:12
  2.8 7.3 %collective-permute-start.1 = (bf16[1,16,8,128]{3,2,1,0:T(8,128)(2,1)S(1)}, bf16[1,16,8,128]{3,2,1,0:T(8,128)(2,1)S(1)}, u32[]{:S(2)}, u32[]{:S(2)}) collective-permute-start(bf16[1,16,8,128]{3,2,1,0:T(8,128)(2,1)S(1)} %get-tuple-element.11), channel_id=1, source_target_pairs={{16,0},{32,16},{48,32},{64,48},{80,64},{96,80},{112,96},{128,112},... | collective-permute-start | bytes 98312 | tf_op jit(solution)/shard_map/ppermute | solution.py:15
  10.2 6.2 %collective-permute-start.2 = (bf16[10,16,1,128]{3,2,1,0:T(2,128)(2,1)S(1)}, bf16[10,16,1,128]{3,2,1,0:T(2,128)(2,1)S(1)}, u32[]{:S(2)}, u32[]{:S(2)}) collective-permute-start(bf16[10,16,1,128]{3,2,1,0:T(2,128)(2,1)S(1)} %get-tuple-element.7), channel_id=1, source_target_pairs={{0,1},{1,2},{2,3},{3,4},{4,5},{5,6},{6,7},{7,8},{8,9},{9,10},{10,1... | collective-permute-start | bytes 122888 | tf_op jit(solution)/shard_map/ppermute | solution.py:12
  14.3 7.8 %collective-permute-start.3 = (bf16[10,16,1,128]{3,2,1,0:T(2,128)(2,1)S(1)}, bf16[10,16,1,128]{3,2,1,0:T(2,128)(2,1)S(1)}, u32[]{:S(2)}, u32[]{:S(2)}) collective-permute-start(bf16[10,16,1,128]{3,2,1,0:T(2,128)(2,1)S(1)} %get-tuple-element.8), channel_id=1, source_target_pairs={{1,0},{2,1},{3,2},{4,3},{5,4},{6,5},{7,6},{8,7},{9,8},{10,9},{11,1... | collective-permute-start | bytes 122888 | tf_op jit(solution)/shard_map/ppermute | solution.py:15
  27.3 9.0 %copy-start.2 = (pred[8,17]{0,1:T(8,128)(4,1)S(1)}, pred[8,17]{0,1:T(8,128)(4,1)}, u32[]{:S(2)}) copy-start(pred[8,17]{0,1:T(8,128)(4,1)} %constant.44) | copy-start | bytes 412
  46.7 22.5 %copy-start.1 = (bf16[64,864]{1,0:T(8,128)(2,1)S(1)}, bf16[64,864]{1,0:T(8,128)(2,1)}, u32[]{:S(2)}) copy-start(bf16[64,864]{1,0:T(8,128)(2,1)} %param.6) | copy-start | bytes 331780
  51.9 7.7 %collective-permute-start.4 = (bf16[1,32,4,64]{1,2,3,0:T(4,128)(2,1)S(1)}, bf16[1,32,4,64]{1,2,3,0:T(4,128)(2,1)S(1)}, u32[]{:S(2)}, u32[]{:S(2)}) collective-permute-start(bf16[1,32,4,64]{1,2,3,0:T(4,128)(2,1)S(1)} %get-tuple-element.9), channel_id=1, source_target_pairs={{0,16},{16,32},{32,48},{48,64},{64,80},{80,96},{96,112},{112,128},... | collective-permute-start | bytes 49160 | tf_op jit(solution)/shard_map/ppermute | solution.py:12
  53.8 7.6 %collective-permute-start.5 = (bf16[1,32,4,64]{1,2,3,0:T(4,128)(2,1)S(1)}, bf16[1,32,4,64]{1,2,3,0:T(4,128)(2,1)S(1)}, u32[]{:S(2)}, u32[]{:S(2)}) collective-permute-start(bf16[1,32,4,64]{1,2,3,0:T(4,128)(2,1)S(1)} %get-tuple-element.10), channel_id=1, source_target_pairs={{16,0},{32,16},{48,32},{64,48},{80,64},{96,80},{112,96},{128,112},... | collective-permute-start | bytes 49160 | tf_op jit(solution)/shard_map/ppermute | solution.py:15
  62.1 11.1 %collective-permute-start.6 = (bf16[6,32,1,64]{1,2,3,0:T(2,128)(2,1)S(1)}, bf16[6,32,1,64]{1,2,3,0:T(2,128)(2,1)S(1)}, u32[]{:S(2)}, u32[]{:S(2)}) collective-permute-start(bf16[6,32,1,64]{1,2,3,0:T(2,128)(2,1)S(1)} %get-tuple-element.5), channel_id=1, source_target_pairs={{0,1},{1,2},{2,3},{3,4},{4,5},{5,6},{6,7},{7,8},{8,9},{9,10},{10,1... | collective-permute-start | bytes 73736 | tf_op jit(solution)/shard_map/ppermute | solution.py:12
  67.9 9.1 %collective-permute-start.7 = (bf16[6,32,1,64]{1,2,3,0:T(2,128)(2,1)S(1)}, bf16[6,32,1,64]{1,2,3,0:T(2,128)(2,1)S(1)}, u32[]{:S(2)}, u32[]{:S(2)}) collective-permute-start(bf16[6,32,1,64]{1,2,3,0:T(2,128)(2,1)S(1)} %get-tuple-element.6), channel_id=1, source_target_pairs={{1,0},{2,1},{3,2},{4,3},{5,4},{6,5},{7,6},{8,7},{9,8},{10,9},{11,1... | collective-permute-start | bytes 73736 | tf_op jit(solution)/shard_map/ppermute | solution.py:15
  77.1 1.1 copy-start.3
  80.3 7.9 %collective-permute-start.8 = (bf16[1,64,2,32]{1,2,3,0:T(2,128)(2,1)S(1)}, bf16[1,64,2,32]{1,2,3,0:T(2,128)(2,1)S(1)}, u32[]{:S(2)}, u32[]{:S(2)}) collective-permute-start(bf16[1,64,2,32]{1,2,3,0:T(2,128)(2,1)S(1)} %get-tuple-element.13), channel_id=1, source_target_pairs={{0,16},{16,32},{32,48},{48,64},{64,80},{80,96},{96,112},{112,128},... | collective-permute-start | bytes 24584 | tf_op jit(solution)/shard_map/ppermute | solution.py:12
  82.2 7.2 %collective-permute-start.9 = (bf16[1,64,2,32]{1,2,3,0:T(2,128)(2,1)S(1)}, bf16[1,64,2,32]{1,2,3,0:T(2,128)(2,1)S(1)}, u32[]{:S(2)}, u32[]{:S(2)}) collective-permute-start(bf16[1,64,2,32]{1,2,3,0:T(2,128)(2,1)S(1)} %get-tuple-element.14), channel_id=1, source_target_pairs={{16,0},{32,16},{48,32},{64,48},{80,64},{96,80},{112,96},{128,112},... | collective-permute-start | bytes 24584 | tf_op jit(solution)/shard_map/ppermute | solution.py:15
  139.2 1.0 copy-start.4
where the time goes:
time: 145 us; the launch traced here: 144 us
  blocking collectives  48.7 us (34%)
  starting transfers between devices  35.4 us (24%)
  local copies, waits for them, and re-layouts  24.6 us (17%)
  waiting for transfers between devices  16.5 us (11%)
  matrix products  11.3 us (8%)
  other arithmetic  7.46 us (5%)
    all_gather x1, blocking collectives, per_device(): whole = lax.all_gather(grown, 'yz', axis=2, tiled=True)  48.7 us
    ppermute x5, starting transfers between devices, with_halo(): lax.ppermute(lax.slice_in_dim(block, 0, width, axis=dim), axis, backward)  19.8 us
    ppermute x5, starting transfers between devices, with_halo(): lax.ppermute(lax.slice_in_dim(block, block.shape[dim] - width, None, axis...  15.5 us
    conv_general_dilated x7, local copies, waits for them, and re-layouts, block_conv(): lax.conv_general_dilated(padded[None], kernel, (1, 1, 1), 'VALID', dimens...  13.2 us
    ppermute x5, waiting for transfers between devices, with_halo(): lax.ppermute(lax.slice_in_dim(block, 0, width, axis=dim), axis, backward)  12.9 us
    conv_general_dilated x3, matrix products, block_conv(): lax.conv_general_dilated(padded[None], kernel, (1, 1, 1), 'VALID', dimens...  11.3 us
    reduce_sum x2, other arithmetic, conv_pool(): return (jnp.sum(grouped, axis=(1, 4, 6)) * 0.125).astype(jnp.bfloat16)  5.47 us
    ppermute x5, waiting for transfers between devices, with_halo(): lax.ppermute(lax.slice_in_dim(block, block.shape[dim] - width, None, axis...  3.6 us
  transfers between devices with their start and end apart: 10, of which 6 were waited for; matrix products, arithmetic and copies ran while one was open for 2% of the time, Pallas kernels for 0%

commit v1 on v0

--- a/solution.py
+++ b/solution.py
@@ -55,7 +55,9 @@
     shards = lax.axis_size("yz")
     out_rows = weight_three.shape[0] // shards
     grown = with_halo(pooled_two, (("gx", 0),), 1)
-    whole = lax.all_gather(grown, "yz", axis=2, tiled=True)
+    whole = jnp.concatenate(
+        lax.all_to_all(jnp.stack([grown] * lax.axis_size("yz")), "yz", 0, 0), axis=2
+    )
     whole = jnp.pad(whole, ((0, 0), (0, 0), (1, 1), (1, 1)))
     picked = lax.dynamic_slice_in_dim(weight_three, lax.axis_index("yz") * out_rows, out_rows, 0)
     summed = jnp.moveaxis(conv_planes(whole, picked), 0, 1)

time: 145 us -> 128 us (0.88)
  the two profiles are of different devices: /device:TPU:2 before, /device:TPU:25 now
where the time goes in v1:
time: 128 us; the launch traced here: 127 us
  waiting for transfers between devices  42.3 us (33%)
  starting transfers between devices  38.9 us (30%)
  local copies, waits for them, and re-layouts  27 us (21%)
  matrix products  11.3 us (9%)
  other arithmetic  7.46 us (6%)
    ppermute x5, waiting for transfers between devices, with_halo(): lax.ppermute(lax.slice_in_dim(block, 0, width, axis=dim), axis, backward)  21.1 us
    ppermute x5, starting transfers between devices, with_halo(): lax.ppermute(lax.slice_in_dim(block, block.shape[dim] - width, None, axis...  19.2 us
    all_to_all x1, waiting for transfers between devices, per_device(): lax.all_to_all(jnp.stack([grown] * lax.axis_size('yz')), 'yz', 0, 0)  16.3 us
    conv_general_dilated x7, local copies, waits for them, and re-layouts, block_conv(): lax.conv_general_dilated(padded[None], kernel, (1, 1, 1), 'VALID', dimens...  13.2 us
    conv_general_dilated x3, matrix products, block_conv(): lax.conv_general_dilated(padded[None], kernel, (1, 1, 1), 'VALID', dimens...  11.3 us
    all_to_all x1, starting transfers between devices, per_device(): lax.all_to_all(jnp.stack([grown] * lax.axis_size('yz')), 'yz', 0, 0)  11.3 us
    ppermute x5, starting transfers between devices, with_halo(): lax.ppermute(lax.slice_in_dim(block, 0, width, axis=dim), axis, backward)  8.35 us
    reduce_sum x2, other arithmetic, conv_pool(): return (jnp.sum(grouped, axis=(1, 4, 6)) * 0.125).astype(jnp.bfloat16)  5.47 us
  transfers between devices with their start and end apart: 11, of which 7 were waited for; matrix products, arithmetic and copies ran while one was open for 2% of the time, Pallas kernels for 0%

profile of v1, /device:TPU:25, one launch (start us, length us, event | category | flops | bytes accessed | tf_op | source)
XLA Modules:
  0.0 127.4 jit_solution(8145035094760275544)
XLA Ops:
  0.8 3.3 %collective-permute-start = (bf16[1,16,8,128]{3,2,1,0:T(8,128)(2,1)S(1)}, bf16[1,16,8,128]{3,2,1,0:T(8,128)(2,1)S(1)}, u32[]{:S(2)}, u32[]{:S(2)}) collective-permute-start(bf16[1,16,8,128]{3,2,1,0:T(8,128)(2,1)S(1)} %get-tuple-element.12), channel_id=1, source_target_pairs={{0,16},{16,32},{32,48},{48,64},{64,80},{80,96},{96,112},{112,128},... | collective-permute-start | bytes 98312 | tf_op jit(solution)/shard_map/ppermute | solution.py:12
  4.2 1.9 %collective-permute-start.1 = (bf16[1,16,8,128]{3,2,1,0:T(8,128)(2,1)S(1)}, bf16[1,16,8,128]{3,2,1,0:T(8,128)(2,1)S(1)}, u32[]{:S(2)}, u32[]{:S(2)}) collective-permute-start(bf16[1,16,8,128]{3,2,1,0:T(8,128)(2,1)S(1)} %get-tuple-element.11), channel_id=1, source_target_pairs={{16,0},{32,16},{48,32},{64,48},{80,64},{96,80},{112,96},{128,112},... | collective-permute-start | bytes 98312 | tf_op jit(solution)/shard_map/ppermute | solution.py:15
  7.1 4.4 %collective-permute-done.1 = bf16[1,16,8,128]{3,2,1,0:T(8,128)(2,1)S(1)} collective-permute-done((bf16[1,16,8,128]{3,2,1,0:T(8,128)(2,1)S(1)}, bf16[1,16,8,128]{3,2,1,0:T(8,128)(2,1)S(1)}, u32[]{:S(2)}, u32[]{:S(2)}) %collective-permute-start.1) | collective-permute-done | bytes 32800 | tf_op jit(solution)/shard_map/ppermute | solution.py:15
  11.6 4.4 %collective-permute-start.2 = (bf16[10,16,1,128]{3,2,1,0:T(2,128)(2,1)S(1)}, bf16[10,16,1,128]{3,2,1,0:T(2,128)(2,1)S(1)}, u32[]{:S(2)}, u32[]{:S(2)}) collective-permute-start(bf16[10,16,1,128]{3,2,1,0:T(2,128)(2,1)S(1)} %get-tuple-element.7), channel_id=1, source_target_pairs={{0,1},{1,2},{2,3},{3,4},{4,5},{5,6},{6,7},{7,8},{8,9},{9,10},{10,1... | collective-permute-start | bytes 122888 | tf_op jit(solution)/shard_map/ppermute | solution.py:12
  16.0 1.3 %collective-permute-start.3 = (bf16[10,16,1,128]{3,2,1,0:T(2,128)(2,1)S(1)}, bf16[10,16,1,128]{3,2,1,0:T(2,128)(2,1)S(1)}, u32[]{:S(2)}, u32[]{:S(2)}) collective-permute-start(bf16[10,16,1,128]{3,2,1,0:T(2,128)(2,1)S(1)} %get-tuple-element.8), channel_id=1, source_target_pairs={{1,0},{2,1},{3,2},{4,3},{5,4},{6,5},{7,6},{8,7},{9,8},{10,9},{11,1... | collective-permute-start | bytes 122888 | tf_op jit(solution)/shard_map/ppermute | solution.py:15
  18.2 4.5 %collective-permute-done.3 = bf16[10,16,1,128]{3,2,1,0:T(2,128)(2,1)S(1)} collective-permute-done((bf16[10,16,1,128]{3,2,1,0:T(2,128)(2,1)S(1)}, bf16[10,16,1,128]{3,2,1,0:T(2,128)(2,1)S(1)}, u32[]{:S(2)}, u32[]{:S(2)}) %collective-permute-start.3) | collective-permute-done | bytes 40992 | tf_op jit(solution)/shard_map/ppermute | solution.py:15
  24.2 3.7 %reshape.69 = bf16[10,16,10,1,8,17]{5,4,2,1,0,3:T(8,128)(2,1)} reshape(bf16[10,16,10,1,136]{4,2,1,0,3:T(8,128)(2,1)S(1)} %pad.15) | data formatting | bytes 870400 | tf_op jit(solution)/shard_map/conv_general_dilated | solution.py:23
  27.9 7.9 %copy.61 = bf16[10,16,10,1,8,17]{1,4,5,2,0,3:T(8,128)(2,1)} copy(bf16[10,16,10,1,8,17]{5,4,2,1,0,3:T(8,128)(2,1)} %reshape.69) | data formatting | bytes 870400 | tf_op jit(solution)/shard_map/conv_general_dilated | solution.py:23
  37.0 7.3 %select_maximum_fusion = f32[8,8,8,17,32]{4,2,3,1,0:T(8,128)S(1)} fusion(pred[8,17]{0,1:T(8,128)(4,1)S(1)} %copy-done.2, bf16[32,3,3,3,16]{0,4,3,2,1:T(8,128)(2,1)S(1)} %bitcast.65, bf16[10,16,10,1,7,2]{1,4,5,2,0,3:T(8,128)(2,1)S(1)} %slice.48, bf16[10,16,10,1,8,17]{1,4,5,2,0,3:T(8,128)(2,1)} %copy.61), kind=kOutput, calls=%fused_computation.2 | convolution fusion | flops 242664448 | bytes 1621896 | tf_op jit(solution)/shard_map/conv_general_dilated | solution.py:23
  45.0 2.2 %slice.49 = f32[8,8,1,128,32]{4,1,3,0,2:T(8,128)} slice(f32[8,8,1,136,32]{4,1,3,0,2:T(8,128)S(1)} %bitcast.53), slice={[0:8], [0:8], [0:1], [0:128], [0:32]} | slice | bytes 2097152 | tf_op jit(solution)/shard_map/jit(relu)/max | solution.py:35
  47.3 5.0 %reduce_sum.18 = f32[4,32,4,64]{1,2,3,0:T(4,128)S(1)} reduce(f32[4,2,32,4,2,64,2]{2,4,3,6,5,1,0:T(2,128)} %bitcast.54, f32[]{:T(128)} %constant.8.clone.1), dimensions={1,4,6}, to_apply=%region_0.1 | reduce | flops 229376 | bytes 1179652 | tf_op jit(solution)/shard_map/reduce_sum | solution.py:38
  52.5 2.7 %collective-permute-start.4 = (bf16[1,32,4,64]{1,2,3,0:T(4,128)(2,1)S(1)}, bf16[1,32,4,64]{1,2,3,0:T(4,128)(2,1)S(1)}, u32[]{:S(2)}, u32[]{:S(2)}) collective-permute-start(bf16[1,32,4,64]{1,2,3,0:T(4,128)(2,1)S(1)} %get-tuple-element.9), channel_id=1, source_target_pairs={{0,16},{16,32},{32,48},{48,64},{64,80},{80,96},{96,112},{112,128},... | collective-permute-start | bytes 49160 | tf_op jit(solution)/shard_map/ppermute | solution.py:12
  55.2 1.9 %collective-permute-start.5 = (bf16[1,32,4,64]{1,2,3,0:T(4,128)(2,1)S(1)}, bf16[1,32,4,64]{1,2,3,0:T(4,128)(2,1)S(1)}, u32[]{:S(2)}, u32[]{:S(2)}) collective-permute-start(bf16[1,32,4,64]{1,2,3,0:T(4,128)(2,1)S(1)} %get-tuple-element.10), channel_id=1, source_target_pairs={{16,0},{32,16},{48,32},{64,48},{80,64},{96,80},{112,96},{128,112},... | collective-permute-start | bytes 49160 | tf_op jit(solution)/shard_map/ppermute | solution.py:15
  57.2 5.8 %collective-permute-done.5 = bf16[1,32,4,64]{1,2,3,0:T(4,128)(2,1)S(1)} collective-permute-done((bf16[1,32,4,64]{1,2,3,0:T(4,128)(2,1)S(1)}, bf16[1,32,4,64]{1,2,3,0:T(4,128)(2,1)S(1)}, u32[]{:S(2)}, u32[]{:S(2)}) %collective-permute-start.5) | collective-permute-done | bytes 16416 | tf_op jit(solution)/shard_map/ppermute | solution.py:15
  63.6 6.1 %collective-permute-start.6 = (bf16[6,32,1,64]{1,2,3,0:T(2,128)(2,1)S(1)}, bf16[6,32,1,64]{1,2,3,0:T(2,128)(2,1)S(1)}, u32[]{:S(2)}, u32[]{:S(2)}) collective-permute-start(bf16[6,32,1,64]{1,2,3,0:T(2,128)(2,1)S(1)} %get-tuple-element.5), channel_id=1, source_target_pairs={{0,1},{1,2},{2,3},{3,4},{4,5},{5,6},{6,7},{7,8},{8,9},{9,10},{10,1... | collective-permute-start | bytes 73736 | tf_op jit(solution)/shard_map/ppermute | solution.py:12
  71.4 4.9 %collective-permute-done.6 = bf16[6,32,1,64]{1,2,3,0:T(2,128)(2,1)S(1)} collective-permute-done((bf16[6,32,1,64]{1,2,3,0:T(2,128)(2,1)S(1)}, bf16[6,32,1,64]{1,2,3,0:T(2,128)(2,1)S(1)}, u32[]{:S(2)}, u32[]{:S(2)}) %collective-permute-start.6) | collective-permute-done | bytes 24608 | tf_op jit(solution)/shard_map/ppermute | solution.py:12
  78.8 1.4 %fusion.36 = f32[4,4,8,9,64]{4,2,3,1,0:T(8,128)S(1)} fusion(bf16[64,3,3,3,32]{0,4,3,2,1:T(8,128)(2,1)S(1)} %bitcast.63, bf16[6,32,6,1,7,2]{1,4,5,2,0,3:T(8,128)(2,1)S(1)} %slice.54, bf16[6,32,6,1,8,9]{1,4,5,2,0,3:T(8,128)(2,1)S(1)} %copy.69, pred[8,9]{0,1:T(8,128)(4,1)S(1)} %copy-done.3), kind=kOutput, calls=%fused_computation.34 | convolution fusion | flops 128157696 | bytes 603720 | tf_op jit(solution)/shard_map/conv_general_dilated | solution.py:23
  80.9 2.7 %collective-permute-start.8 = (bf16[1,64,2,32]{1,2,3,0:T(2,128)(2,1)S(1)}, bf16[1,64,2,32]{1,2,3,0:T(2,128)(2,1)S(1)}, u32[]{:S(2)}, u32[]{:S(2)}) collective-permute-start(bf16[1,64,2,32]{1,2,3,0:T(2,128)(2,1)S(1)} %get-tuple-element.13), channel_id=1, source_target_pairs={{0,16},{16,32},{32,48},{48,64},{64,80},{80,96},{96,112},{112,128},... | collective-permute-start | bytes 24584 | tf_op jit(solution)/shard_map/ppermute | solution.py:12
  83.7 1.9 %collective-permute-start.9 = (bf16[1,64,2,32]{1,2,3,0:T(2,128)(2,1)S(1)}, bf16[1,64,2,32]{1,2,3,0:T(2,128)(2,1)S(1)}, u32[]{:S(2)}, u32[]{:S(2)}) collective-permute-start(bf16[1,64,2,32]{1,2,3,0:T(2,128)(2,1)S(1)} %get-tuple-element.14), channel_id=1, source_target_pairs={{16,0},{32,16},{48,32},{64,48},{80,64},{96,80},{112,96},{128,112},... | collective-permute-start | bytes 24584 | tf_op jit(solution)/shard_map/ppermute | solution.py:15
  85.6 5.2 %collective-permute-done.9 = bf16[1,64,2,32]{1,2,3,0:T(2,128)(2,1)S(1)} collective-permute-done((bf16[1,64,2,32]{1,2,3,0:T(2,128)(2,1)S(1)}, bf16[1,64,2,32]{1,2,3,0:T(2,128)(2,1)S(1)}, u32[]{:S(2)}, u32[]{:S(2)}) %collective-permute-start.9) | collective-permute-done | bytes 8224 | tf_op jit(solution)/shard_map/ppermute | solution.py:15
  91.2 1.5 %reshape.70 = bf16[16,2,8192]{2,1,0:T(2,128)(2,1)} reshape(bf16[16,4,2,32,64]{4,3,2,1,0:T(8,128)(2,1)S(1)} %broadcast_bitcast_fusion) | data formatting | bytes 1048576
  92.7 11.3 %all-to-all-start = ((bf16[16,2,8192]{2,1,0:T(2,128)(2,1)}), bf16[16,2,8192]{2,1,0:T(2,128)(2,1)S(1)}, u32[]{:S(2)}, u32[]{:S(2)}) async-start(bf16[16,2,8192]{2,1,0:T(2,128)(2,1)} %reshape.70), calls=%async_computation | async-start | bytes 1048576 | tf_op jit(solution)/shard_map/all_to_all | solution.py:59
  104.2 16.3 %all-to-all-done = bf16[16,2,8192]{2,1,0:T(2,128)(2,1)S(1)} async-done(((bf16[16,2,8192]{2,1,0:T(2,128)(2,1)}), bf16[16,2,8192]{2,1,0:T(2,128)(2,1)S(1)}, u32[]{:S(2)}, u32[]{:S(2)}) %all-to-all-start) | async-done | bytes 524320 | tf_op jit(solution)/shard_map/all_to_all | solution.py:59
  123.3 2.7 %fusion.30 = bf16[2,32,8,5,8]{4,2,3,1,0:T(8,128)(2,1)S(1)} fusion(bf16[8,3,3,3,64]{0,4,3,2,1:T(8,128)(2,1)S(1)} %bitcast.62, bf16[4,64,34,1,7,2]{1,4,5,2,0,3:T(8,128)(2,1)S(1)} %slice.58, bf16[4,64,34,1,8,5]{1,4,5,2,0,3:T(8,128)(2,1)S(1)} %copy.76, pred[8,5]{0,1:T(8,128)(4,1)S(1)} %copy-done.4), kind=kOutput, calls=%fused_computation.29 | convolution fusion | flops 73764864 | bytes 1008680 | tf_op jit(solution)/shard_map/conv_general_dilated | solution.py:23
  (60 shorter events, 16.6 us)
Async XLA Ops:
  0.0 104.1 %copy-start = (bf16[128,1728]{0,1:T(8,128)(2,1)S(1)}, bf16[128,1728]{0,1:T(8,128)(2,1)}, u32[]{:S(2)}) copy-start(bf16[128,1728]{0,1:T(8,128)(2,1)} %param.7) | copy-start | bytes 1327108
  0.8 5.3 %collective-permute-start = (bf16[1,16,8,128]{3,2,1,0:T(8,128)(2,1)S(1)}, bf16[1,16,8,128]{3,2,1,0:T(8,128)(2,1)S(1)}, u32[]{:S(2)}, u32[]{:S(2)}) collective-permute-start(bf16[1,16,8,128]{3,2,1,0:T(8,128)(2,1)S(1)} %get-tuple-element.12), channel_id=1, source_target_pairs={{0,16},{16,32},{32,48},{48,64},{64,80},{80,96},{96,112},{112,128},... | collective-permute-start | bytes 98312 | tf_op jit(solution)/shard_map/ppermute | solution.py:12
  4.2 7.3 %collective-permute-start.1 = (bf16[1,16,8,128]{3,2,1,0:T(8,128)(2,1)S(1)}, bf16[1,16,8,128]{3,2,1,0:T(8,128)(2,1)S(1)}, u32[]{:S(2)}, u32[]{:S(2)}) collective-permute-start(bf16[1,16,8,128]{3,2,1,0:T(8,128)(2,1)S(1)} %get-tuple-element.11), channel_id=1, source_target_pairs={{16,0},{32,16},{48,32},{64,48},{80,64},{96,80},{112,96},{128,112},... | collective-permute-start | bytes 98312 | tf_op jit(solution)/shard_map/ppermute | solution.py:15
  11.6 6.6 %collective-permute-start.2 = (bf16[10,16,1,128]{3,2,1,0:T(2,128)(2,1)S(1)}, bf16[10,16,1,128]{3,2,1,0:T(2,128)(2,1)S(1)}, u32[]{:S(2)}, u32[]{:S(2)}) collective-permute-start(bf16[10,16,1,128]{3,2,1,0:T(2,128)(2,1)S(1)} %get-tuple-element.7), channel_id=1, source_target_pairs={{0,1},{1,2},{2,3},{3,4},{4,5},{5,6},{6,7},{7,8},{8,9},{9,10},{10,1... | collective-permute-start | bytes 122888 | tf_op jit(solution)/shard_map/ppermute | solution.py:12
  16.0 6.7 %collective-permute-start.3 = (bf16[10,16,1,128]{3,2,1,0:T(2,128)(2,1)S(1)}, bf16[10,16,1,128]{3,2,1,0:T(2,128)(2,1)S(1)}, u32[]{:S(2)}, u32[]{:S(2)}) collective-permute-start(bf16[10,16,1,128]{3,2,1,0:T(2,128)(2,1)S(1)} %get-tuple-element.8), channel_id=1, source_target_pairs={{1,0},{2,1},{3,2},{4,3},{5,4},{6,5},{7,6},{8,7},{9,8},{10,9},{11,1... | collective-permute-start | bytes 122888 | tf_op jit(solution)/shard_map/ppermute | solution.py:15
  27.9 9.0 %copy-start.2 = (pred[8,17]{0,1:T(8,128)(4,1)S(1)}, pred[8,17]{0,1:T(8,128)(4,1)}, u32[]{:S(2)}) copy-start(pred[8,17]{0,1:T(8,128)(4,1)} %constant.44) | copy-start | bytes 412
  47.3 23.7 %copy-start.1 = (bf16[64,864]{1,0:T(8,128)(2,1)S(1)}, bf16[64,864]{1,0:T(8,128)(2,1)}, u32[]{:S(2)}) copy-start(bf16[64,864]{1,0:T(8,128)(2,1)} %param.6) | copy-start | bytes 331780
  52.5 4.7 %collective-permute-start.4 = (bf16[1,32,4,64]{1,2,3,0:T(4,128)(2,1)S(1)}, bf16[1,32,4,64]{1,2,3,0:T(4,128)(2,1)S(1)}, u32[]{:S(2)}, u32[]{:S(2)}) collective-permute-start(bf16[1,32,4,64]{1,2,3,0:T(4,128)(2,1)S(1)} %get-tuple-element.9), channel_id=1, source_target_pairs={{0,16},{16,32},{32,48},{48,64},{64,80},{80,96},{96,112},{112,128},... | collective-permute-start | bytes 49160 | tf_op jit(solution)/shard_map/ppermute | solution.py:12
  55.2 7.7 %collective-permute-start.5 = (bf16[1,32,4,64]{1,2,3,0:T(4,128)(2,1)S(1)}, bf16[1,32,4,64]{1,2,3,0:T(4,128)(2,1)S(1)}, u32[]{:S(2)}, u32[]{:S(2)}) collective-permute-start(bf16[1,32,4,64]{1,2,3,0:T(4,128)(2,1)S(1)} %get-tuple-element.10), channel_id=1, source_target_pairs={{16,0},{32,16},{48,32},{64,48},{80,64},{96,80},{112,96},{128,112},... | collective-permute-start | bytes 49160 | tf_op jit(solution)/shard_map/ppermute | solution.py:15
  63.6 12.7 %collective-permute-start.6 = (bf16[6,32,1,64]{1,2,3,0:T(2,128)(2,1)S(1)}, bf16[6,32,1,64]{1,2,3,0:T(2,128)(2,1)S(1)}, u32[]{:S(2)}, u32[]{:S(2)}) collective-permute-start(bf16[6,32,1,64]{1,2,3,0:T(2,128)(2,1)S(1)} %get-tuple-element.5), channel_id=1, source_target_pairs={{0,1},{1,2},{2,3},{3,4},{4,5},{5,6},{6,7},{7,8},{8,9},{9,10},{10,1... | collective-permute-start | bytes 73736 | tf_op jit(solution)/shard_map/ppermute | solution.py:12
  69.7 7.9 %collective-permute-start.7 = (bf16[6,32,1,64]{1,2,3,0:T(2,128)(2,1)S(1)}, bf16[6,32,1,64]{1,2,3,0:T(2,128)(2,1)S(1)}, u32[]{:S(2)}, u32[]{:S(2)}) collective-permute-start(bf16[6,32,1,64]{1,2,3,0:T(2,128)(2,1)S(1)} %get-tuple-element.6), channel_id=1, source_target_pairs={{1,0},{2,1},{3,2},{4,3},{5,4},{6,5},{7,6},{8,7},{9,8},{10,9},{11,1... | collective-permute-start | bytes 73736 | tf_op jit(solution)/shard_map/ppermute | solution.py:15
  77.7 1.1 copy-start.3
  80.9 4.6 %collective-permute-start.8 = (bf16[1,64,2,32]{1,2,3,0:T(2,128)(2,1)S(1)}, bf16[1,64,2,32]{1,2,3,0:T(2,128)(2,1)S(1)}, u32[]{:S(2)}, u32[]{:S(2)}) collective-permute-start(bf16[1,64,2,32]{1,2,3,0:T(2,128)(2,1)S(1)} %get-tuple-element.13), channel_id=1, source_target_pairs={{0,16},{16,32},{32,48},{48,64},{64,80},{80,96},{96,112},{112,128},... | collective-permute-start | bytes 24584 | tf_op jit(solution)/shard_map/ppermute | solution.py:12
  83.7 7.2 %collective-permute-start.9 = (bf16[1,64,2,32]{1,2,3,0:T(2,128)(2,1)S(1)}, bf16[1,64,2,32]{1,2,3,0:T(2,128)(2,1)S(1)}, u32[]{:S(2)}, u32[]{:S(2)}) collective-permute-start(bf16[1,64,2,32]{1,2,3,0:T(2,128)(2,1)S(1)} %get-tuple-element.14), channel_id=1, source_target_pairs={{16,0},{32,16},{48,32},{64,48},{80,64},{96,80},{112,96},{128,112},... | collective-permute-start | bytes 24584 | tf_op jit(solution)/shard_map/ppermute | solution.py:15
  92.7 27.8 %all-to-all-start = ((bf16[16,2,8192]{2,1,0:T(2,128)(2,1)}), bf16[16,2,8192]{2,1,0:T(2,128)(2,1)S(1)}, u32[]{:S(2)}, u32[]{:S(2)}) async-start(bf16[16,2,8192]{2,1,0:T(2,128)(2,1)} %reshape.70), calls=%async_computation | async-start | bytes 1048576 | tf_op jit(solution)/shard_map/all_to_all | solution.py:59
  122.2 1.0 copy-start.4
